TPU v7x, 128 devices: a whole 4x4x4 slice. The times are simulated.
128 devices in a mesh: leaf: 4 (over y), row: 8 (over z, core), col: 4 (over x).
Axes of the slice: x: 4, y: 4, z: 4, core: 2. Of those that a mesh axis runs over, the one named last changes fastest.
Arguments:
- sigma_top: float32 [1024, 1024], P(('leaf', 'row'), 'col')
- panels: float32 [4, 7, 1024, 512], P('leaf', None, 'row', 'col'), may hold values from -0.1875 to 0.1875
- inverse_diag: float32 [4, 7, 512, 512], P('leaf', None, 'col')
- slot_lists: int32 [4, 6, 8], P('leaf'), may hold values from -1 to 11, as said below
- parent_links: int32 [4, 4], P('leaf'), may hold values from 1 to 2
Outputs:
- ancestor_block: float32 [4, 7, 1024, 512], P('leaf', None, 'row', 'col')
- diagonal_block: float32 [4, 7, 512, 512], P('leaf', None, None, 'col')
Inputs may be any that keep to these rules, and one draw needn't show every extreme that they name: `slot_lists`: in every row, entries 0 to 3 are 8 to 11 in order (the parent's own tiles); then come 1 to 3 distinct parent ancestor slots, below 8 for supernodes 1 and 2 and below 4 for supernodes 3 to 6; the rest are -1, so every row has padding. `parent_links`: each supernode 3 to 6 has supernode 1 or 2 as its parent. `sigma_top`: symmetric.
All inputs are finite; a program needn't handle non-finite values.
Results may differ from a plain program's by a relative error of at most 0.0001.
Values sent between devices are 32-bit elements; how exact they have to be, the bound alone decides.
A program may use at most 128 MiB of HBM per device.

v0:
```python
import jax
import jax.numpy as jnp
from jax import lax
from jax.sharding import PartitionSpec as P

TILE = 128
HIGHEST = lax.Precision.HIGHEST


def mm(a, b):
    return jnp.matmul(a, b, precision=HIGHEST, preferred_element_type=jnp.float32)


def tile_rows(matrix, index, tile):
    return lax.dynamic_slice_in_dim(matrix, index * tile, tile, 0)


def tile_cols(matrix, index, tile):
    return lax.dynamic_slice_in_dim(matrix, index * tile, tile, 1)


def scatter_factor(factor_col, slots, positions, tile):
    tiles = factor_col.reshape(slots.shape[0], tile, factor_col.shape[1])
    hits = slots[:, None] == jnp.arange(positions, dtype=slots.dtype)[None, :]
    present = jnp.any(hits, axis=0)
    source = jnp.argmax(hits, axis=0)
    moved = jnp.take(tiles, source, axis=0)
    moved = jnp.where(present[:, None, None], moved, 0.0)
    return moved.reshape(positions * tile, factor_col.shape[1])


def pick_transposed(column_block, picks, tile):
    tiles = column_block.reshape(-1, tile, tile)
    chosen = jnp.take(tiles, jnp.maximum(picks, 0), axis=0)
    chosen = jnp.where((picks >= 0)[:, None, None], chosen, 0.0)
    return jnp.transpose(chosen, (2, 0, 1)).reshape(tile, picks.shape[0] * tile)


def body(sigma_top, panels, inverse_diag, slot_lists, parent_links):
    tile = TILE
    row_count = lax.axis_size("row")
    col_count = lax.axis_size("col")
    leaf_count = lax.axis_size("leaf")
    r = lax.axis_index("row")
    c = lax.axis_index("col")
    panel = panels[0]
    inverse = inverse_diag[0]
    picks_all = slot_lists[0]
    parents = parent_links[0]
    nodes = panel.shape[0]
    width = inverse.shape[2]
    own_tiles = width // tile
    slot_count = picks_all.shape[1]
    positions = slot_count + own_tiles
    band = width // row_count
    partial_factor = mm(panel, inverse)
    factor_rows = lax.psum(partial_factor, "col")
    living = jnp.concatenate([jnp.ones((1, slot_count), jnp.bool_), picks_all >= 0], axis=0)
    live_here = jnp.take(living, r, axis=1).astype(jnp.float32)
    factor_rows = factor_rows * live_here[:, None, None]
    factor_tile = lax.dynamic_slice_in_dim(factor_rows, c * tile, tile, 2)
    factor_cols = lax.all_gather(factor_tile, "row", axis=1, tiled=True)
    inverse_band = lax.dynamic_slice_in_dim(inverse, r * band, band, 2)
    partial_gram = mm(jnp.transpose(inverse_band, (0, 2, 1)), inverse)
    gram_piece = lax.psum_scatter(partial_gram, "col", scatter_dimension=2, tiled=True)
    local_rows, local_cols = sigma_top.shape
    gathered = lax.all_gather(sigma_top, ("leaf", "row", "col"), axis=0)
    sigma = gathered.reshape(leaf_count * row_count, col_count, local_rows, local_cols)
    sigma = jnp.transpose(sigma, (0, 2, 1, 3)).reshape(
        leaf_count * row_count * local_rows, col_count * local_cols
    )

    def diag_partial(first, products):
        rows = factor_rows[first : first + products.shape[0]]
        return mm(jnp.transpose(rows, (0, 2, 1)), products)

    def reduce_and_gather(first, products):
        count = products.shape[0]
        piece = lax.psum_scatter(
            diag_partial(first, products), "row", scatter_dimension=1, tiled=True
        )
        piece = piece + gram_piece[first : first + count]
        both = jnp.concatenate([products, piece], axis=1)
        everything = lax.all_gather(both, ("row", "col"), axis=0)
        everything = everything.reshape(row_count, col_count, count, tile + band, tile)
        product_full = jnp.transpose(everything[:, :, :, :tile], (2, 0, 3, 1, 4)).reshape(
            count, row_count * tile, col_count * tile
        )
        diag_full = jnp.transpose(everything[:, :, :, tile:], (2, 0, 3, 1, 4)).reshape(
            count, row_count * band, col_count * tile
        )
        return (product_full, diag_full)

    own_row = jnp.minimum(r, own_tiles - 1)
    upper = r < own_tiles
    product_0 = mm(tile_rows(sigma, r, tile), factor_cols[0])
    product_full_0, diag_full_0 = reduce_and_gather(0, product_0[None])
    product_full_0 = product_full_0[0]
    diag_full_0 = diag_full_0[0]
    level_1 = []
    for node in (1, 2):
        slots = picks_all[node - 1]
        spread = scatter_factor(factor_cols[node], slots, positions, tile)
        top_row = jnp.concatenate(
            [
                -jnp.transpose(tile_cols(product_full_0, own_row, tile)),
                tile_rows(diag_full_0, own_row, tile),
            ],
            axis=1,
        )
        source = slots[jnp.maximum(r, own_tiles)]
        source_row = jnp.maximum(source, 0)
        low_row = jnp.concatenate(
            [tile_rows(sigma, source_row, tile), -tile_rows(product_full_0, source_row, tile)],
            axis=1,
        )
        low_row = jnp.where(source >= 0, low_row, 0.0)
        row = jnp.where(upper, top_row, low_row)
        level_1.append(mm(row, spread))
    product_1 = jnp.stack(level_1)
    product_full_1, diag_full_1 = reduce_and_gather(1, product_1)
    level_2 = []
    for node in range(3, nodes):
        slots = picks_all[node - 1]
        parent = parents[node - 3] - 1
        parent_slots = jnp.take(picks_all, parent, axis=0)
        product_p = jnp.take(product_full_1, parent, axis=0)
        diag_p = jnp.take(diag_full_1, parent, axis=0)
        spread = scatter_factor(factor_cols[node], slots, positions, tile)
        top_row = jnp.concatenate(
            [-jnp.transpose(tile_cols(product_p, own_row, tile)), tile_rows(diag_p, own_row, tile)],
            axis=1,
        )
        source = slots[jnp.maximum(r, own_tiles)]
        source_row = jnp.clip(source, 0, own_tiles - 1)
        corner = pick_transposed(
            -tile_cols(product_full_0, source_row, tile), parent_slots[own_tiles:], tile
        )
        low_row = jnp.concatenate(
            [
                tile_rows(diag_full_0, source_row, tile),
                corner,
                -tile_rows(product_p, source_row, tile),
            ],
            axis=1,
        )
        low_row = jnp.where(source >= 0, low_row, 0.0)
        row = jnp.where(upper, top_row, low_row)
        level_2.append(mm(row, spread))
    product_2 = jnp.stack(level_2)
    first_2 = 3
    count_2 = product_2.shape[0]
    gram_rows = jnp.zeros((count_2, width, tile), jnp.float32)
    gram_rows = lax.dynamic_update_slice_in_dim(
        gram_rows, gram_piece[first_2 : first_2 + count_2], r * band, 1
    )
    diag_2 = lax.psum(diag_partial(first_2, product_2) + gram_rows, "row")
    products = jnp.concatenate([product_0[None], product_1, product_2], axis=0)
    diag_cols = jnp.concatenate(
        [
            tile_cols(diag_full_0, c, tile)[None],
            lax.dynamic_slice_in_dim(diag_full_1, c * tile, tile, 2),
            diag_2,
        ],
        axis=0,
    )
    return ((-products)[None], diag_cols[None])


def solution(mesh):
    return jax.shard_map(
        body,
        mesh=mesh,
        in_specs=(
            P(("leaf", "row"), "col"),
            P("leaf", None, "row", "col"),
            P("leaf", None, "col", None),
            P("leaf", None, None),
            P("leaf", None),
        ),
        out_specs=(P("leaf", None, "row", "col"), P("leaf", None, None, "col")),
        check_vma=False,
    )
```

profile of v0, /device:TPU:0, one launch (start us, length us, event | category | flops | bytes accessed | tf_op | source)
XLA Modules:
  0.0 459.2 jit_solution(14943117877159287603)
XLA Ops:
  8.1 1.4 copy-done
  9.5 3.9 fusion.2
  14.3 57.6 %all-reduce.4.cloned.1.call-done = f32[7,128,512]{2,1,0:T(8,128)} async-done(((f32[7,128,512]{2,1,0:T(8,128)}), f32[7,128,512]{2,1,0:T(8,128)}) %all-reduce.4.cloned.1.call-update) | async-done | bytes 1835024 | tf_op jit(solution)/shard_map/psum | solution.py:57
  72.0 1.8 broadcast_multiply_fusion
  73.7 1.2 copy-done.2
  75.9 2.3 fusion
  78.3 18.1 %all-gather.10.cloned.1.call-done = f32[4096,256]{1,0:T(8,128)} async-done(((f32[32,256]{1,0:T(8,128)}), f32[4096,256]{1,0:T(8,128)}) %all-gather.10.cloned.1.call-update) | async-done | bytes 4194320 | tf_op jit(solution)/shard_map/all_gather | solution.py:67
  96.3 5.8 %copy.83 = f32[32,4,32,256]{3,1,2,0:T(4,128)S(1)} copy(f32[32,4,32,256]{3,2,1,0:T(8,128)} %bitcast.194) | data formatting | bytes 8388608 | tf_op jit(solution)/shard_map/reshape | solution.py:68
  102.2 3.0 copy.124
  105.1 20.2 %all-gather.8.cloned.1.call-done = f32[7,1024,128]{2,1,0:T(8,128)} async-done(((f32[7,128,128]{2,1,0:T(8,128)}), f32[7,1024,128]{2,1,0:T(8,128)}) %all-gather.8.cloned.1.call-update) | async-done | bytes 3670032 | tf_op jit(solution)/shard_map/all_gather | solution.py:62
  125.3 2.5 bitcast_dynamic-update-slice_fusion.6
  127.8 1.3 convolution_bitcast_fusion
  129.2 30.5 %reduce-scatter.4.cloned.1.call-done = f32[1,64,128]{2,1,0:T(8,128)} async-done(((f32[1,512,128]{2,1,0:T(8,128)}), f32[1,64,128]{2,1,0:T(8,128)}) %reduce-scatter.4.cloned.1.call-update) | async-done | bytes 32784 | tf_op jit(solution)/shard_map/reduce_scatter | solution.py:79
  170.4 3.1 fusion.102
  173.5 1.5 gather_fusion.1
  175.0 1.5 gather_fusion
  176.4 2.3 select_select_fusion.4
  179.7 2.3 constant_dynamic-slice_fusion.22
  182.0 23.9 %all-gather.12.cloned.1.call-done = f32[32,192,128]{2,1,0:T(8,128)} async-done(((f32[1,192,128]{2,1,0:T(8,128)}), f32[32,192,128]{2,1,0:T(8,128)}) %all-gather.12.cloned.1.call-update) | async-done | bytes 3145744 | tf_op jit(solution)/shard_map/all_gather | solution.py:84
  206.0 1.3 slice.190
  207.3 3.2 slice.189
  210.5 2.9 copy.114
  213.3 2.1 copy.133
  217.1 1.4 dynamic-slice_negate_fusion
  219.5 1.8 copy.117
  221.3 1.7 neg.74
  224.9 2.9 bitcast_dynamic-update-slice_fusion.5
  227.8 1.6 bitcast_dynamic-update-slice_fusion.4
  229.4 1.8 fusion.71
  231.2 30.5 %reduce-scatter.8.cloned.1.call-done = f32[2,64,128]{2,1,0:T(8,128)} async-done(((f32[2,512,128]{2,1,0:T(8,128)}), f32[2,64,128]{2,1,0:T(8,128)}) %reduce-scatter.8.cloned.1.call-update) | async-done | bytes 65552 | tf_op jit(solution)/shard_map/reduce_scatter | solution.py:79
  270.7 1.3 iota_reduce_fusion.3
  271.9 1.2 iota_reduce_fusion.2
  274.2 2.5 gather_fusion.7
  276.8 1.5 gather_fusion.9
  278.3 1.5 gather_fusion.5
  280.4 2.3 select_select_fusion.1
  285.9 1.9 copy.123
  287.8 2.1 copy.108
  290.8 1.7 gather_fusion.6
  293.7 1.3 gather_fusion.4
  299.2 12.6 %all-gather.14.cloned.1.call-done = f32[64,192,128]{2,1,0:T(8,128)} async-done(((f32[2,192,128]{2,1,0:T(8,128)}), f32[64,192,128]{2,1,0:T(8,128)}) %all-gather.14.cloned.1.call-update) | async-done | bytes 6291472 | tf_op jit(solution)/shard_map/all_gather | solution.py:84
  311.9 3.2 slice.195
  315.0 4.7 %slice.194 = f32[8,4,2,128,128]{4,3,2,1,0:T(8,128)} slice(f32[8,4,2,192,128]{4,3,2,1,0:T(8,128)} %bitcast.193), slice={[0:8], [0:4], [0:2], [0:128], [0:128]} | slice | bytes 8388608 | tf_op jit(solution)/shard_map/slice | solution.py:86
  319.8 5.3 %copy.118 = f32[8,4,2,128,128]{3,0,4,1,2:T(8,128)} copy(f32[8,4,2,128,128]{4,3,2,1,0:T(8,128)} %slice.194) | data formatting | bytes 8388608
  325.0 4.9 %reshape.293 = f32[2,1024,512]{1,2,0:T(8,128)} reshape(f32[2,8,128,4,128]{2,1,4,3,0:T(8,128)} %bitcast.183) | data formatting | bytes 8388608 | tf_op jit(solution)/shard_map/reshape | solution.py:86
  329.9 4.3 copy.134
  334.2 3.1 reshape.294
  337.3 4.2 select_bitcast_fusion.4
  345.8 7.9 %select_bitcast_fusion = (f32[1024,512]{0,1:T(8,128)}, f32[1,1024,512]{1,2,0:T(8,128)}, f32[1,1024,512]{1,2,0:T(8,128)}, f32[1,1024,512]{1,2,0:T(8,128)}) fusion(f32[2,1024,512]{1,2,0:T(8,128)} %reshape.293, s32[]{:T(128)S(6)} %select_n.346, pred[]{:T(512)S(6)} %and.78, s32[]{:T(128)S(6)} %select_n.326, s32[]{:T(128)S(6)} %select_n.316, s32[]{:T(128)S(6)} %select_n.336), kind=kLoop, calls=%fused_computation.12 | loop fusion | flops 524288 | bytes 16777232 | tf_op jit(solution)/shard_map/jit(_take)/select_n | solution.py:127
  353.6 2.9 copy.121
  356.6 1.9 select_bitcast_fusion.2
  360.5 1.9 negate_bitcast_fusion
  363.7 3.0 copy.119
  366.7 1.9 select_bitcast_fusion.3
  370.6 2.9 copy.122
  373.5 1.9 select_bitcast_fusion.1
  377.5 3.3 bitcast_dynamic-update-slice_fusion.3
  380.8 1.6 bitcast_dynamic-update-slice_fusion.2
  382.4 1.6 bitcast_dynamic-update-slice_fusion.1
  384.0 1.6 bitcast_dynamic-update-slice_fusion
  385.6 1.8 fusion.62
  390.2 1.2 constant_dynamic-slice_fusion.8
  391.4 57.6 %all-reduce.6.cloned.1.call-done = f32[4,512,128]{2,1,0:T(8,128)} async-done(((f32[4,512,128]{2,1,0:T(8,128)}), f32[4,512,128]{2,1,0:T(8,128)}) %all-reduce.6.cloned.1.call-update) | async-done | bytes 1048592 | tf_op jit(solution)/shard_map/psum | solution.py:157
  449.1 2.6 maximum_bitcast_fusion
  (185 shorter events, 42.8 us)
Async XLA Ops:
  8.0 1.5 copy-start
  8.0 6.0 %copy-start.37 = (s32[1,6,8]{2,0,1:T(1,128)S(1)}, s32[1,6,8]{2,0,1:T(1,128)}, u32[]{:S(2)}) copy-start(s32[1,6,8]{2,0,1:T(1,128)} %param.18) | copy-start | bytes 580
  8.0 63.9 %all-reduce.4.cloned.1.call-start = ((), (), s32[]{:S(2)}) async-start(), calls=%async_computation.3 | async-start | bytes 3670016 | tf_op jit(solution)/shard_map/psum | solution.py:57
  13.4 82.9 %all-gather.10.cloned.1.call-start = ((), (), s32[]{:S(2)}) async-start(), calls=%async_computation.9 | async-start | bytes 4227072 | tf_op jit(solution)/shard_map/all_gather | solution.py:67
  14.0 111.3 %all-gather.8.cloned.1.call-start = ((), (), s32[]{:S(2)}) async-start(), calls=%async_computation.4 | async-start | bytes 4128768 | tf_op jit(solution)/shard_map/all_gather | solution.py:62
  73.7 1.2 copy-start.2
  75.8 53.4 %reduce-scatter.6.cloned.1.call-start = ((), (), s32[]{:S(2)}) async-start(), calls=%async_computation.6 | async-start | bytes 1146880 | tf_op jit(solution)/shard_map/reduce_scatter | solution.py:65
  78.2 81.5 %reduce-scatter.4.cloned.1.call-start = ((), (), s32[]{:S(2)}) async-start(), calls=%async_computation.5 | async-start | bytes 294912 | tf_op jit(solution)/shard_map/reduce_scatter | solution.py:79
  102.1 25.6 %copy-start.3 = (f32[7,128,512]{2,1,0:T(8,128)S(1)}, f32[7,128,512]{2,1,0:T(8,128)}, u32[]{:S(2)}) copy-start(f32[7,128,512]{2,1,0:T(8,128)} %copy-done.2) | copy-start | bytes 5505028
  129.1 76.9 %all-gather.12.cloned.1.call-start = ((), (), s32[]{:S(2)}) async-start(), calls=%async_computation.10 | async-start | bytes 3244032 | tf_op jit(solution)/shard_map/all_gather | solution.py:84
  161.2 100.5 %reduce-scatter.8.cloned.1.call-start = ((), (), s32[]{:S(2)}) async-start(), calls=%async_computation.7 | async-start | bytes 589824 | tf_op jit(solution)/shard_map/reduce_scatter | solution.py:79
  176.4 2.3 copy-start.12
  216.2 2.3 copy-start.5
  223.8 4.0 copy-start.16
  223.8 4.0 copy-start.21
  223.8 4.0 copy-start.30
  229.4 34.2 %copy-start.38 = (s32[1,4]{1,0:T(1,128)S(1)}, s32[1,4]{1,0:T(1,128)}, u32[]{:S(2)}) copy-start(s32[1,4]{1,0:T(1,128)} %param.19) | copy-start | bytes 52
  229.4 47.4 %copy-start.7 = (f32[1,1024,128]{2,1,0:T(8,128)S(1)}, f32[1,1024,128]{2,1,0:T(8,128)}, u32[]{:S(2)}) copy-start(f32[1,1024,128]{2,1,0:T(8,128)} %get-tuple-element.69) | copy-start | bytes 1572868
  231.2 47.1 %copy-start.6 = (f32[1,1024,128]{2,1,0:T(8,128)S(1)}, f32[1,1024,128]{2,1,0:T(8,128)}, u32[]{:S(2)}) copy-start(f32[1,1024,128]{2,1,0:T(8,128)} %get-tuple-element.71) | copy-start | bytes 1572868
  231.2 80.7 %all-gather.14.cloned.1.call-start = ((), (), s32[]{:S(2)}) async-start(), calls=%async_computation.11 | async-start | bytes 6488064 | tf_op jit(solution)/shard_map/all_gather | solution.py:84
  263.3 185.8 %all-reduce.6.cloned.1.call-start = ((), (), s32[]{:S(2)}) async-start(), calls=%async_computation.8 | async-start | bytes 2097152 | tf_op jit(solution)/shard_map/psum | solution.py:157
  280.4 2.3 copy-start.11
  280.4 3.4 copy-start.10
  283.8 6.0 %copy-start.19 = (f32[1024,128]{0,1:T(8,128)S(1)}, f32[1024,128]{0,1:T(8,128)}, u32[]{:S(2)}) copy-start(f32[1024,128]{0,1:T(8,128)} %get-tuple-element.76) | copy-start | bytes 1572868
  285.9 7.6 %copy-start.18 = (f32[1024,128]{0,1:T(8,128)S(1)}, f32[1024,128]{0,1:T(8,128)}, u32[]{:S(2)}) copy-start(f32[1024,128]{0,1:T(8,128)} %get-tuple-element.77) | copy-start | bytes 1572868
  290.8 6.0 %copy-start.17 = (f32[1024,128]{0,1:T(8,128)S(1)}, f32[1024,128]{0,1:T(8,128)}, u32[]{:S(2)}) copy-start(f32[1024,128]{0,1:T(8,128)} %get-tuple-element.78) | copy-start | bytes 1572868
  293.7 4.9 %copy-start.22 = (f32[1024,128]{1,0:T(8,128)S(1)}, f32[1024,128]{1,0:T(8,128)}, u32[]{:S(2)}) copy-start(f32[1024,128]{1,0:T(8,128)} %copy.108) | copy-start | bytes 1572868
  356.6 2.7 copy-start.34
  359.3 4.1 copy-start.31
  366.7 2.7 copy-start.33
  373.5 2.7 copy-start.32
  377.4 3.4 copy-start.8
  377.4 3.4 copy-start.15
  377.4 3.4 copy-start.24
  377.4 3.4 copy-start.26
  377.4 3.4 copy-start.29
  377.4 5.0 %copy-start.9 = (f32[128,1536]{1,0:T(8,128)S(1)}, f32[128,1536]{1,0:T(8,128)}, u32[]{:S(2)}) copy-start(f32[128,1536]{1,0:T(8,128)} %copy.106) | copy-start | bytes 2359300
  377.4 5.0 %copy-start.14 = (f32[12,128,128]{2,1,0:T(8,128)S(1)}, f32[12,128,128]{2,1,0:T(8,128)}, u32[]{:S(2)}) copy-start(f32[12,128,128]{2,1,0:T(8,128)} %select_select_fusion.1) | copy-start | bytes 2359300
  377.4 5.0 %copy-start.23 = (f32[128,512]{1,0:T(8,128)S(1)}, f32[128,512]{1,0:T(8,128)}, u32[]{:S(2)}) copy-start(f32[128,512]{1,0:T(8,128)} %get-tuple-element.87) | copy-start | bytes 786436
  377.4 5.0 %copy-start.27 = (f32[128,512]{1,0:T(8,128)S(1)}, f32[128,512]{1,0:T(8,128)}, u32[]{:S(2)}) copy-start(f32[128,512]{1,0:T(8,128)} %dynamic-slice_negate_fusion.5) | copy-start | bytes 786436
  377.4 5.0 %copy-start.28 = (f32[128,512]{1,0:T(8,128)S(1)}, f32[128,512]{1,0:T(8,128)}, u32[]{:S(2)}) copy-start(f32[128,512]{1,0:T(8,128)} %copy.105) | copy-start | bytes 786436
  380.8 3.2 copy-start.13
  380.8 3.2 copy-start.20
  380.8 3.2 copy-start.25
  385.6 1.8 copy-start.36
  387.4 2.0 copy-start.35
  387.4 1.0 copy-start.4
  390.2 61.4 %copy-start.1 = (f32[1,7,128,512]{3,2,1,0:T(8,128)S(1)}, f32[1,7,128,512]{3,2,1,0:T(8,128)}, u32[]{:S(2)}) copy-start(f32[1,7,128,512]{3,2,1,0:T(8,128)} %param.17) | copy-start | bytes 5505028
Sparse Core Ops, SparseCore 0:
  13.5 58.3 all-reduce.3
  79.1 22.6 reduce-scatter.5
  129.2 30.4 reduce-scatter.3
  162.1 43.8 all-gather.11
  231.3 30.3 reduce-scatter.7
  263.8 48.0 all-gather.13
Sparse Core Ops, SparseCore 1:
  17.0 79.3 all-gather.9
  98.5 26.8 all-gather.7
  388.5 60.5 all-reduce.5
where the time goes:
time: 461 us; the launch traced here: 459 us
  waiting for transfers between devices  252 us (55%)
  local copies, waits for them, and re-layouts  100 us (22%)
  other arithmetic  53.9 us (12%)
  between operations  26.5 us (6%)
  matrix products  26 us (6%)
    reduce_scatter x2, waiting for transfers between devices, reduce_and_gather(): lax.psum_scatter(diag_partial(first, products), 'row', scatter_dimension=...  61 us
    psum x1, waiting for transfers between devices, body(): factor_rows = lax.psum(partial_factor, 'col')  57.6 us
    psum x1, waiting for transfers between devices, body(): diag_2 = lax.psum(diag_partial(first_2, product_2) + gram_rows, 'row')  57.6 us
    all_gather x2, waiting for transfers between devices, reduce_and_gather(): everything = lax.all_gather(both, ('row', 'col'), axis=0)  36.5 us
    unnamed x92, local copies, waits for them, and re-layouts  35.4 us
    dot_general x12, matrix products, mm(): jnp.matmul(a, b, precision=HIGHEST, preferred_element_type=jnp.float32)  26 us
    all_gather x1, waiting for transfers between devices, body(): factor_cols = lax.all_gather(factor_tile, 'row', axis=1, tiled=True)  20.2 us
    all_gather x1, waiting for transfers between devices, body(): gathered = lax.all_gather(sigma_top, ('leaf', 'row', 'col'), axis=0)  18.1 us
  transfers between devices with their start and end apart: 9, of which 8 were waited for; matrix products, arithmetic and copies ran while one was open for 15% of the time, Pallas kernels for 0%

commit v1 on v0

--- a/solution.py
+++ b/solution.py
@@ -54,7 +54,8 @@
     positions = slot_count + own_tiles
     band = width // row_count
     partial_factor = mm(panel, inverse)
-    factor_rows = lax.psum(partial_factor, "col")
+    parts = lax.all_gather(partial_factor, "col")
+    factor_rows = jnp.sum(parts, axis=0)
     living = jnp.concatenate([jnp.ones((1, slot_count), jnp.bool_), picks_all >= 0], axis=0)
     live_here = jnp.take(living, r, axis=1).astype(jnp.float32)
     factor_rows = factor_rows * live_here[:, None, None]

time: 461 us -> 553 us (1.20)
  waiting for transfers between devices: 252 us -> 337 us
  other arithmetic: 53.9 us -> 60.2 us
    all_gather x0 -> x1, waiting for transfers between devices: none -> 75.9 us  [body(): parts = lax.all_gather(partial_factor, 'col')]
    psum x1 -> x0, waiting for transfers between devices: 57.6 us -> none  [body(): factor_rows = lax.psum(partial_factor, 'col')]
    all_gather x1, waiting for transfers between devices: 18.1 us -> 56.6 us  [body(): gathered = lax.all_gather(sigma_top, ('leaf', 'row', 'col'), axis=0)]
    reduce_scatter x1, waiting for transfers between devices: 0.02 us -> 22.6 us  [body(): lax.psum_scatter(partial_gram, 'col', scatter_dimension=2, tiled=True)]
    unnamed x92 -> x96, local copies, waits for them, and re-layouts: 35.4 us -> 35.4 us
  transfers between devices with their start and end apart: 9 -> 9, of which waited for: 8 -> 9; matrix products, arithmetic and copies ran while one was open for 15% -> 14% of each run, Pallas kernels for 0% -> 0%
where the time goes in v1:
time: 553 us; the launch traced here: 551 us
  waiting for transfers between devices  337 us (61%)
  local copies, waits for them, and re-layouts  104 us (19%)
  other arithmetic  60.2 us (11%)
  between operations  24.9 us (5%)
  matrix products  24.4 us (4%)
    all_gather x1, waiting for transfers between devices, body(): parts = lax.all_gather(partial_factor, 'col')  75.9 us
    reduce_scatter x2, waiting for transfers between devices, reduce_and_gather(): lax.psum_scatter(diag_partial(first, products), 'row', scatter_dimension=...  63.8 us
    psum x1, waiting for transfers between devices, body(): diag_2 = lax.psum(diag_partial(first_2, product_2) + gram_rows, 'row')  57.9 us
    all_gather x1, waiting for transfers between devices, body(): gathered = lax.all_gather(sigma_top, ('leaf', 'row', 'col'), axis=0)  56.6 us
    unnamed x96, local copies, waits for them, and re-layouts  35.4 us
    all_gather x2, waiting for transfers between devices, reduce_and_gather(): everything = lax.all_gather(both, ('row', 'col'), axis=0)  34.4 us
    all_gather x1, waiting for transfers between devices, body(): factor_cols = lax.all_gather(factor_tile, 'row', axis=1, tiled=True)  25.1 us
    dot_general x12, matrix products, mm(): jnp.matmul(a, b, precision=HIGHEST, preferred_element_type=jnp.float32)  24.4 us
  transfers between devices with their start and end apart: 9, of which 9 were waited for; matrix products, arithmetic and copies ran while one was open for 14% of the time, Pallas kernels for 0%

profile of v1, /device:TPU:0, one launch (start us, length us, event | category | flops | bytes accessed | tf_op | source)
XLA Modules:
  0.0 551.4 jit_solution(5935152266696628289)
XLA Ops:
  7.2 1.4 copy-done
  8.7 3.9 fusion.2
  13.7 75.9 %all-gather.14.cloned.1.call-done = f32[28,128,512]{2,1,0:T(8,128)} async-done(((f32[7,128,512]{2,1,0:T(8,128)}), f32[28,128,512]{2,1,0:T(8,128)}) %all-gather.14.cloned.1.call-update) | async-done | bytes 7340048 | tf_op jit(solution)/shard_map/all_gather | solution.py:57
  89.6 5.4 reduce_sum.9
  95.0 2.7 copy.91
  97.7 1.7 broadcast_multiply_fusion
  99.4 1.2 copy-done.2
  101.5 2.2 fusion
  103.8 56.6 %all-gather.12.cloned.1.call-done = f32[4096,256]{1,0:T(8,128)} async-done(((f32[32,256]{1,0:T(8,128)}), f32[4096,256]{1,0:T(8,128)}) %all-gather.12.cloned.1.call-update) | async-done | bytes 4194320 | tf_op jit(solution)/shard_map/all_gather | solution.py:68
  160.4 5.8 %copy.90 = f32[32,4,32,256]{3,1,2,0:T(4,128)S(1)} copy(f32[32,4,32,256]{3,2,1,0:T(8,128)} %bitcast.196) | data formatting | bytes 8388608 | tf_op jit(solution)/shard_map/reshape | solution.py:69
  166.2 3.0 copy.140
  169.2 25.1 %all-gather.10.cloned.1.call-done = f32[7,1024,128]{1,2,0:T(8,128)} async-done(((f32[7,128,128]{1,2,0:T(8,128)}), f32[7,1024,128]{1,2,0:T(8,128)}) %all-gather.10.cloned.1.call-update) | async-done | bytes 3670032 | tf_op jit(solution)/shard_map/all_gather | solution.py:63
  194.3 2.4 bitcast_dynamic-update-slice_fusion.6
  197.8 22.6 %reduce-scatter.6.cloned.1.call-done = f32[7,64,128]{2,1,0:T(8,128)} async-done(((f32[7,64,512]{2,1,0:T(8,128)}), f32[7,64,128]{2,1,0:T(8,128)}) %reduce-scatter.6.cloned.1.call-update) | async-done | bytes 229392 | tf_op jit(solution)/shard_map/reduce_scatter | solution.py:66
  220.4 33.3 %reduce-scatter.4.cloned.1.call-done = f32[1,64,128]{2,1,0:T(8,128)} async-done(((f32[1,512,128]{2,1,0:T(8,128)}), f32[1,64,128]{2,1,0:T(8,128)}) %reduce-scatter.4.cloned.1.call-update) | async-done | bytes 32784 | tf_op jit(solution)/shard_map/reduce_scatter | solution.py:80
  264.5 2.3 constant_dynamic-slice_fusion.22
  266.8 3.3 fusion.102
  270.5 1.5 gather_fusion.1
  272.6 2.2 select_select_fusion.4
  275.9 24.1 %all-gather.16.cloned.1.call-done = f32[32,192,128]{2,1,0:T(8,128)} async-done(((f32[1,192,128]{2,1,0:T(8,128)}), f32[32,192,128]{2,1,0:T(8,128)}) %all-gather.16.cloned.1.call-update) | async-done | bytes 3145744 | tf_op jit(solution)/shard_map/all_gather | solution.py:85
  299.9 1.3 slice.190
  301.2 3.2 slice.189
  304.4 2.9 copy.130
  307.3 2.1 copy.149
  311.0 1.4 dynamic-slice_negate_fusion
  314.3 1.8 neg.74
  316.1 1.8 copy.132
  318.9 2.9 bitcast_dynamic-update-slice_fusion.5
  321.8 1.6 bitcast_dynamic-update-slice_fusion.4
  323.4 1.4 fusion.71
  324.8 30.5 %reduce-scatter.8.cloned.1.call-done = f32[2,64,128]{2,1,0:T(8,128)} async-done(((f32[2,512,128]{2,1,0:T(8,128)}), f32[2,64,128]{2,1,0:T(8,128)}) %reduce-scatter.8.cloned.1.call-update) | async-done | bytes 65552 | tf_op jit(solution)/shard_map/reduce_scatter | solution.py:80
  364.5 1.3 iota_reduce_fusion.3
  369.5 1.2 copy.125
  370.7 2.5 gather_fusion.9
  373.2 1.5 gather_fusion.7
  374.7 1.5 gather_fusion.5
  376.2 1.5 gather_fusion.3
  377.7 2.4 select_select_fusion
  383.2 1.9 copy.139
  386.3 1.3 gather_fusion.6
  389.7 1.3 gather_fusion.4
  395.3 10.3 %all-gather.18.cloned.1.call-done = f32[64,192,128]{2,1,0:T(8,128)} async-done(((f32[2,192,128]{2,1,0:T(8,128)}), f32[64,192,128]{2,1,0:T(8,128)}) %all-gather.18.cloned.1.call-update) | async-done | bytes 6291472 | tf_op jit(solution)/shard_map/all_gather | solution.py:85
  405.6 3.2 slice.195
  408.8 4.7 slice.194
  413.5 5.3 copy.134
  418.8 4.9 reshape.293
  423.6 4.3 copy.150
  428.0 3.1 reshape.294
  431.1 4.2 select_bitcast_fusion.4
  439.5 7.9 %select_bitcast_fusion = (f32[1024,512]{0,1:T(8,128)}, f32[1,1024,512]{1,2,0:T(8,128)}, f32[1,1024,512]{1,2,0:T(8,128)}, f32[1,1024,512]{1,2,0:T(8,128)}) fusion(f32[2,1024,512]{1,2,0:T(8,128)} %reshape.293, s32[]{:T(128)S(6)} %select_n.346, pred[]{:T(512)S(6)} %and.78, s32[]{:T(128)S(6)} %select_n.326, s32[]{:T(128)S(6)} %select_n.316, s32[]{:T(128)S(6)} %select_n.336), kind=kLoop, calls=%fused_computation.12 | loop fusion | flops 524288 | bytes 16777232 | tf_op jit(solution)/shard_map/jit(_take)/select_n | solution.py:128
  447.4 2.9 copy.137
  450.3 1.9 select_bitcast_fusion.2
  454.2 1.9 negate_bitcast_fusion
  457.5 3.0 copy.135
  460.4 1.9 select_bitcast_fusion.3
  464.3 2.9 copy.138
  467.2 1.9 select_bitcast_fusion.1
  471.2 3.3 bitcast_dynamic-update-slice_fusion.3
  474.6 1.6 bitcast_dynamic-update-slice_fusion.2
  476.2 1.6 bitcast_dynamic-update-slice_fusion.1
  477.8 1.6 bitcast_dynamic-update-slice_fusion
  483.2 1.2 constant_dynamic-slice_fusion.8
  484.4 57.9 %all-reduce.3.cloned.1.call-done = f32[4,512,128]{2,1,0:T(8,128)} async-done(((f32[4,512,128]{2,1,0:T(8,128)}), f32[4,512,128]{2,1,0:T(8,128)}) %all-reduce.3.cloned.1.call-update) | async-done | bytes 1048592 | tf_op jit(solution)/shard_map/psum | solution.py:158
  542.3 2.6 maximum_bitcast_fusion
  (197 shorter events, 49.1 us)
Async XLA Ops:
  7.2 1.5 copy-start
  7.2 6.2 %copy-start.39 = (s32[1,6,8]{2,0,1:T(1,128)S(1)}, s32[1,6,8]{2,0,1:T(1,128)}, u32[]{:S(2)}) copy-start(s32[1,6,8]{2,0,1:T(1,128)} %param.18) | copy-start | bytes 580
  7.2 82.4 %all-gather.14.cloned.1.call-start = ((), (), s32[]{:S(2)}) async-start(), calls=%async_computation.9 | async-start | bytes 9175040 | tf_op jit(solution)/shard_map/all_gather | solution.py:57
  12.6 147.9 %all-gather.12.cloned.1.call-start = ((), (), s32[]{:S(2)}) async-start(), calls=%async_computation.8 | async-start | bytes 4227072 | tf_op jit(solution)/shard_map/all_gather | solution.py:68
  13.3 181.0 %all-gather.10.cloned.1.call-start = ((), (), s32[]{:S(2)}) async-start(), calls=%async_computation.3 | async-start | bytes 4128768 | tf_op jit(solution)/shard_map/all_gather | solution.py:63
  99.4 1.2 copy-start.2
  101.5 118.9 %reduce-scatter.6.cloned.1.call-start = ((), (), s32[]{:S(2)}) async-start(), calls=%async_computation.5 | async-start | bytes 1146880 | tf_op jit(solution)/shard_map/reduce_scatter | solution.py:66
  103.8 149.9 %reduce-scatter.4.cloned.1.call-start = ((), (), s32[]{:S(2)}) async-start(), calls=%async_computation.4 | async-start | bytes 294912 | tf_op jit(solution)/shard_map/reduce_scatter | solution.py:80
  166.2 30.5 %copy-start.3 = (f32[7,128,512]{1,2,0:T(8,128)S(1)}, f32[7,128,512]{1,2,0:T(8,128)}, u32[]{:S(2)}) copy-start(f32[7,128,512]{1,2,0:T(8,128)} %copy-done.2) | copy-start | bytes 5505028
  197.8 102.1 %all-gather.16.cloned.1.call-start = ((), (), s32[]{:S(2)}) async-start(), calls=%async_computation.10 | async-start | bytes 3244032 | tf_op jit(solution)/shard_map/all_gather | solution.py:85
  255.1 100.2 %reduce-scatter.8.cloned.1.call-start = ((), (), s32[]{:S(2)}) async-start(), calls=%async_computation.6 | async-start | bytes 589824 | tf_op jit(solution)/shard_map/reduce_scatter | solution.py:80
  310.1 2.4 copy-start.5
  314.3 7.5 %copy-start.14 = (f32[12,128,128]{2,1,0:T(8,128)S(1)}, f32[12,128,128]{2,1,0:T(8,128)}, u32[]{:S(2)}) copy-start(f32[12,128,128]{2,1,0:T(8,128)} %select_select_fusion.4) | copy-start | bytes 2359300
  317.9 3.9 copy-start.22
  317.9 3.9 copy-start.32
  323.4 33.8 %copy-start.40 = (s32[1,4]{1,0:T(1,128)S(1)}, s32[1,4]{1,0:T(1,128)}, u32[]{:S(2)}) copy-start(s32[1,4]{1,0:T(1,128)} %param.19) | copy-start | bytes 52
  323.4 44.7 %copy-start.19 = (f32[1,1024,128]{1,2,0:T(8,128)S(1)}, f32[1,1024,128]{1,2,0:T(8,128)}, u32[]{:S(2)}) copy-start(f32[1,1024,128]{1,2,0:T(8,128)} %get-tuple-element.69) | copy-start | bytes 1572868
  323.4 45.7 %copy-start.18 = (f32[1,1024,128]{1,2,0:T(8,128)S(1)}, f32[1,1024,128]{1,2,0:T(8,128)}, u32[]{:S(2)}) copy-start(f32[1,1024,128]{1,2,0:T(8,128)} %get-tuple-element.70) | copy-start | bytes 1572868
  324.7 44.5 %copy-start.17 = (f32[1,1024,128]{1,2,0:T(8,128)S(1)}, f32[1,1024,128]{1,2,0:T(8,128)}, u32[]{:S(2)}) copy-start(f32[1,1024,128]{1,2,0:T(8,128)} %get-tuple-element.71) | copy-start | bytes 1572868
  324.8 80.8 %all-gather.18.cloned.1.call-start = ((), (), s32[]{:S(2)}) async-start(), calls=%async_computation.11 | async-start | bytes 6488064 | tf_op jit(solution)/shard_map/all_gather | solution.py:85
  356.9 185.5 %all-reduce.3.cloned.1.call-start = ((), (), s32[]{:S(2)}) async-start(), calls=%async_computation.7 | async-start | bytes 2097152 | tf_op jit(solution)/shard_map/psum | solution.py:158
  377.7 2.4 copy-start.10
  377.7 3.5 copy-start.9
  377.7 4.5 copy-start.8
  381.1 4.0 copy-start.21
  381.1 5.0 copy-start.20
  383.2 6.2 %copy-start.16 = (f32[1024,128]{0,1:T(8,128)S(1)}, f32[1024,128]{0,1:T(8,128)}, u32[]{:S(2)}) copy-start(f32[1024,128]{0,1:T(8,128)} %get-tuple-element.77) | copy-start | bytes 1572868
  386.3 6.6 %copy-start.15 = (f32[1024,128]{0,1:T(8,128)S(1)}, f32[1024,128]{0,1:T(8,128)}, u32[]{:S(2)}) copy-start(f32[1024,128]{0,1:T(8,128)} %get-tuple-element.78) | copy-start | bytes 1572868
  389.7 4.9 copy-start.24
  450.3 2.7 copy-start.36
  453.0 4.1 copy-start.33
  460.4 2.7 copy-start.35
  467.2 2.7 copy-start.34
  471.1 3.4 copy-start.6
  471.1 3.4 copy-start.13
  471.1 3.4 copy-start.26
  471.1 3.4 copy-start.28
  471.1 3.4 copy-start.31
  471.2 5.0 copy-start.7
  471.2 5.0 copy-start.12
  471.2 5.0 copy-start.25
  471.2 5.0 copy-start.29
  471.2 5.0 copy-start.30
  474.6 3.2 copy-start.11
  474.6 3.2 copy-start.23
  474.6 3.2 copy-start.27
  479.3 1.0 copy-start.38
  480.4 2.0 copy-start.37
  480.4 1.0 copy-start.4
  483.2 61.7 %copy-start.1 = (f32[1,7,128,512]{3,2,1,0:T(8,128)S(1)}, f32[1,7,128,512]{3,2,1,0:T(8,128)}, u32[]{:S(2)}) copy-start(f32[1,7,128,512]{3,2,1,0:T(8,128)} %param.17) | copy-start | bytes 5505028
Sparse Core Ops, SparseCore 0:
  12.7 76.8 all-gather.13
  92.7 67.6 all-gather.11
  162.7 31.5 all-gather.9
  196.6 23.7 reduce-scatter.5
  223.2 30.4 reduce-scatter.3
  256.0 43.8 all-gather.15
  324.9 30.3 reduce-scatter.7
  357.5 48.0 all-gather.17
  481.5 60.7 all-reduce.2
